TPU v7x, 256 devices: a whole 4x4x8 slice. The times are simulated.
256 devices in a mesh: gx: 32 (over z, x), gy: 8 (over y, core).
Axes of the slice: x: 4, y: 4, z: 8, core: 2. Of those that a mesh axis runs over, the one named last changes fastest.
Arguments:
- right_side: float32 [8192, 512], P(('gx', 'gy')), may hold values from -6 to 6
- diagonal: float32 [8192, 512], P(('gx', 'gy')), may hold values from 0.5 to 2
- features: float32 [8192, 64, 512], P(('gx', 'gy')), may hold values from -0.078125 to 0.078125
- neighbours: int32 [8192, 27], P(('gx', 'gy')), may hold values from -1 to 8191, as said below
- vertex_features: float32 [64, 262144], P(None, ('gx', 'gy')), may hold values from -0.75 to 0.75
- vertex_bricks: int32 [262144], P(('gx', 'gy')), may hold values from 0 to 8191, as said below
Outputs:
- solution_field: float32 [8192, 512], P(('gx', 'gy'))
- residual: float32 [8192, 512], P(('gx', 'gy'))
- vertex_values: float32 [262144], P(('gx', 'gy'))
Inputs may be any that keep to these rules, and one draw needn't show every extreme that they name: `neighbours`: bricks sit at distinct integer brick coordinates; slot k of a row names the brick at the offset (k // 9 - 1, k // 3 % 3 - 1, k % 3 - 1) from its own, or -1 where no brick is there, so slot 13 names the brick itself and the relation is symmetric. Every brick whose coordinates differ from a brick's by at most two in each direction is held by a device whose gx and gy indices each differ from that brick's holder's by at most one. `vertex_bricks`: vertex n names a brick of its own gx slab: a brick from (n // 8192) * 256 to (n // 8192) * 256 + 255.
All inputs are finite; a program needn't handle non-finite values.
Results may differ from a plain program's by a relative error of at most 0.0002.
Values sent between devices are 32-bit elements; how exact they have to be, the bound alone decides.
No kernel may reach another device: no remote copies, remote signals or barrier semaphores. Data moves between devices by JAX's collectives and lax.ppermute only.
A program may use at most 64 MiB of HBM per device.

v0:
```python
import jax
import jax.numpy as jnp
from jax import lax
from jax.sharding import PartitionSpec as P

ITERS = 3


def with_halo(cells, sides, width):
    for axis, dim in sides:
        count = lax.axis_size(axis)
        ends = count - 1
        head = lax.slice_in_dim(cells, 0, width, axis=dim)
        tail = lax.slice_in_dim(cells, cells.shape[dim] - width, cells.shape[dim], axis=dim)
        cells = jnp.concatenate(
            [
                lax.ppermute(tail, axis, [(i, (i + 1) % count) for i in range(ends)]),
                cells,
                lax.ppermute(head, axis, [((i + 1) % count, i) for i in range(ends)]),
            ],
            axis=dim,
        )
    return cells


def coefficient(features, field):
    return jnp.einsum("bfv,bv->bf", features, field, precision=lax.Precision.HIGHEST)


def squares(values):
    return lax.psum(jnp.sum(values * values), ("gx", "gy"))


def per_device(right_side, diagonal, features, neighbours, vertex_features, vertex_bricks):
    nrows = features.shape[0]
    width = features.shape[1]
    across = lax.axis_size("gy")
    row_index = lax.axis_index("gx")
    col_index = lax.axis_index("gy")
    targets = jnp.arange(9 * nrows, dtype=jnp.int32)
    valid = neighbours >= 0
    safe_ids = jnp.where(valid, neighbours, 0)
    owner = safe_ids // nrows
    offset_x = owner // across - row_index + 1
    offset_y = owner % across - col_index + 1
    inside = valid & (offset_x >= 0) & (offset_x < 3) & (offset_y >= 0) & (offset_y < 3)
    position, inside = ((offset_x * 3 + offset_y) * nrows + safe_ids % nrows, inside)
    hits = (position[:, :, None] == targets[None, None, :]) & inside[:, :, None]
    counts = jnp.sum(hits.astype(jnp.float32), axis=1)

    def first_halo(values):
        cycle = with_halo(values.reshape(1, 1, nrows, width), (("gx", 0), ("gy", 1)), 1)
        return cycle.reshape(9 * nrows, width)

    def first_sum(values):
        return jnp.dot(counts, first_halo(values), precision=lax.Precision.HIGHEST)

    solution_field = jnp.zeros_like(right_side)
    residual = right_side
    direction = right_side
    norm_now = squares(residual)
    for step in range(ITERS):
        second_cycle = with_halo(
            first_sum(coefficient(features, direction)).reshape(1, 1, nrows, width),
            (("gx", 0), ("gy", 1)),
            1,
        )
        second = jnp.dot(
            counts, second_cycle.reshape(9 * nrows, width), precision=lax.Precision.HIGHEST
        )
        image = diagonal * direction + jnp.einsum(
            "bfv,bf->bv", features, second, precision=lax.Precision.HIGHEST
        )
        alpha = norm_now / lax.psum(jnp.sum(direction * image), ("gx", "gy"))
        solution_field = solution_field + alpha * direction
        residual = residual - alpha * image
        norm_next = squares(residual)
        direction = residual + norm_next / norm_now * direction
        norm_now = norm_next
    surface = first_sum(coefficient(features, solution_field))
    slab_rows = lax.all_gather(surface, "gy", axis=0, tiled=True)
    local_ids = vertex_bricks - row_index * across * nrows
    picked = jnp.take(slab_rows, local_ids, axis=0)
    vertex_values = jnp.sum(vertex_features * picked.T, axis=0)
    return (solution_field, residual, vertex_values)


def solution(mesh):
    placed = (
        P(("gx", "gy"), None),
        P(("gx", "gy"), None),
        P(("gx", "gy"), None, None),
        P(("gx", "gy"), None),
        P(None, ("gx", "gy")),
        P(("gx", "gy")),
    )
    return jax.shard_map(
        per_device,
        mesh=mesh,
        in_specs=placed,
        out_specs=(P(("gx", "gy"), None), P(("gx", "gy"), None), P(("gx", "gy"))),
        check_vma=False,
    )
```

profile of v0, /device:TPU:129, one launch (start us, length us, event | category | flops | bytes accessed | tf_op | source)
XLA Modules:
  0.0 560.7 jit_solution(662496368784365687)
XLA Ops:
  0.7 5.8 %fusion.8 = f32[32,1,64]{2,1,0:T(1,128)S(1)} fusion(f32[32,64,512]{2,1,0:T(8,128)} %param.8, f32[32,512,1]{1,0,2:T(8,128)} %bitcast.92), kind=kOutput, calls=%fused_computation.25 | convolution fusion | flops 12582912 | bytes 4268032 | tf_op jit(solution)/shard_map/bfv,bv->bf/dot_general | solution.py:27
  6.5 3.9 collective-permute-start.1
  10.4 1.9 collective-permute-start
  12.7 5.6 collective-permute-done
  18.2 4.0 collective-permute-start.3
  22.3 3.1 collective-permute-start.2
  25.4 0.3 convert_reduce_fusion
  25.7 0.8 collective-permute-done.2
  26.8 1.9 collective-permute-start.5
  28.7 3.4 collective-permute-start.4
  32.1 4.4 collective-permute-done.4
  36.5 2.1 collective-permute-start.7
  38.6 5.2 collective-permute-start.6
  43.8 1.1 collective-permute-done.6
  45.2 4.3 fusion.25
  49.5 0.6 multiply_reduce_fusion.4
  50.2 74.5 %all-reduce = (f32[]{:T(128)}, f32[]{:T(128)}) all-reduce(f32[]{:T(128)} %get-tuple-element.4, f32[]{:T(128)} %get-tuple-element.3), channel_id=1, replica_groups=mesh['gx'=32,'gy'=8] {'gx','gy'}, use_global_device_ids=true, to_apply=%region_1.2 | all-reduce | flops 2 | bytes 16 | tf_op jit(solution)/shard_map/psum | solution.py:31
  126.0 0.6 multiply_reduce_fusion.3
  126.7 73.5 %psum.44 = f32[]{:T(128)} all-reduce(f32[]{:T(128)} %get-tuple-element.9), channel_id=1, replica_groups=mesh['gx'=32,'gy'=8] {'gx','gy'}, use_global_device_ids=true, to_apply=%region_6.7 | all-reduce | flops 1 | bytes 8 | tf_op jit(solution)/shard_map/psum | solution.py:31
  201.5 5.4 fusion.6
  206.9 3.8 collective-permute-start.9
  210.8 1.9 collective-permute-start.8
  212.7 5.9 %collective-permute-done.8 = f32[1,1,32,64]{3,2,1,0:T(8,128)S(1)} collective-permute-done((f32[1,1,32,64]{3,2,1,0:T(8,128)S(1)}, f32[1,1,32,64]{3,2,1,0:T(8,128)S(1)}, u32[]{:S(2)}, u32[]{:S(2)}) %collective-permute-start.8) | collective-permute-done | bytes 8224 | tf_op jit(solution)/shard_map/ppermute | solution.py:17
  218.6 4.0 collective-permute-start.11
  222.6 1.9 collective-permute-start.10
  224.5 1.2 collective-permute-done.10
  226.0 1.9 collective-permute-start.13
  227.9 3.4 collective-permute-start.12
  231.3 4.4 collective-permute-done.12
  235.7 3.2 collective-permute-start.15
  238.9 4.3 collective-permute-start.14
  243.2 1.0 collective-permute-done.14
  244.4 2.1 fusion.27
  246.5 0.6 multiply_reduce_fusion.2
  247.1 73.2 %psum.45 = f32[]{:T(128)} all-reduce(f32[]{:T(128)} %multiply_reduce_fusion.2), channel_id=1, replica_groups=mesh['gx'=32,'gy'=8] {'gx','gy'}, use_global_device_ids=true, to_apply=%region_8.9 | all-reduce | flops 1 | bytes 8 | tf_op jit(solution)/shard_map/psum | solution.py:74
  321.7 0.6 multiply_reduce_fusion.1
  322.3 73.3 %psum.46 = f32[]{:T(128)} all-reduce(f32[]{:T(128)} %get-tuple-element.7), channel_id=1, replica_groups=mesh['gx'=32,'gy'=8] {'gx','gy'}, use_global_device_ids=true, to_apply=%region_10.11 | all-reduce | flops 1 | bytes 8 | tf_op jit(solution)/shard_map/psum | solution.py:31
  397.0 5.4 fusion.4
  402.4 4.2 collective-permute-start.17
  406.6 1.9 collective-permute-start.16
  408.6 5.9 %collective-permute-done.16 = f32[1,1,32,64]{3,2,1,0:T(8,128)S(1)} collective-permute-done((f32[1,1,32,64]{3,2,1,0:T(8,128)S(1)}, f32[1,1,32,64]{3,2,1,0:T(8,128)S(1)}, u32[]{:S(2)}, u32[]{:S(2)}) %collective-permute-start.16) | collective-permute-done | bytes 8224 | tf_op jit(solution)/shard_map/ppermute | solution.py:17
  414.5 4.0 collective-permute-start.19
  418.5 1.9 collective-permute-start.18
  420.4 1.2 collective-permute-done.18
  421.8 1.9 collective-permute-start.21
  423.7 3.4 collective-permute-start.20
  427.1 4.4 collective-permute-done.20
  431.6 3.2 collective-permute-start.23
  434.8 4.1 collective-permute-start.22
  438.9 1.1 collective-permute-done.22
  440.3 2.1 fusion.29
  442.4 0.6 multiply_reduce_fusion
  443.0 73.2 %psum.47 = f32[]{:T(128)} all-reduce(f32[]{:T(128)} %multiply_reduce_fusion), channel_id=1, replica_groups=mesh['gx'=32,'gy'=8] {'gx','gy'}, use_global_device_ids=true, to_apply=%region_12.13 | all-reduce | flops 1 | bytes 8 | tf_op jit(solution)/shard_map/psum | solution.py:74
  517.5 0.7 multiply_subtract_fusion
  518.2 5.3 fusion.2
  523.5 3.7 collective-permute-start.25
  527.2 1.9 collective-permute-start.24
  529.2 5.8 %collective-permute-done.24 = f32[1,1,32,64]{3,2,1,0:T(8,128)S(1)} collective-permute-done((f32[1,1,32,64]{3,2,1,0:T(8,128)S(1)}, f32[1,1,32,64]{3,2,1,0:T(8,128)S(1)}, u32[]{:S(2)}, u32[]{:S(2)}) %collective-permute-start.24) | collective-permute-done | bytes 8224 | tf_op jit(solution)/shard_map/ppermute | solution.py:17
  535.0 4.0 collective-permute-start.27
  539.0 3.4 collective-permute-start.26
  542.7 0.9 collective-permute-done.26
  543.8 13.1 %all_gather.3 = f32[256,64]{1,0:T(8,128)S(1)} all-gather(f32[32,64]{1,0:T(8,128)S(1)} %fusion.30), channel_id=1, replica_groups=mesh['gx'=32,'gy'=8] {'gy'}, dimensions={0}, use_global_device_ids=true | all-gather | bytes 73728 | tf_op jit(solution)/shard_map/all_gather | solution.py:81
  556.9 2.8 gather_fusion
  559.7 1.0 fusion.1
  (60 shorter events, 2.2 us)
Async XLA Ops:
  0.6 11.7 %copy-start.6 = (s32[32,27]{1,0:T(8,128)S(1)}, s32[32,27]{1,0:T(8,128)}, u32[]{:S(2)}) copy-start(s32[32,27]{1,0:T(8,128)} %param.9) | copy-start | bytes 10372
  0.6 48.9 %copy-start.2 = (f32[32,512]{1,0:T(8,128)S(1)}, f32[32,512]{1,0:T(8,128)}, u32[]{:S(2)}) copy-start(f32[32,512]{1,0:T(8,128)} %param.7) | copy-start | bytes 196612
  0.7 48.9 %copy-start.3 = (f32[32,512]{1,0:T(8,128)S(1)}, f32[32,512]{1,0:T(8,128)}, u32[]{:S(2)}) copy-start(f32[32,512]{1,0:T(8,128)} %param.6) | copy-start | bytes 196612
  6.5 6.2 %collective-permute-start.1 = (f32[1,1,32,64]{3,2,1,0:T(8,128)S(1)}, f32[1,1,32,64]{3,2,1,0:T(8,128)S(1)}, u32[]{:S(2)}, u32[]{:S(2)}) collective-permute-start(f32[1,1,32,64]{3,2,1,0:T(8,128)S(1)} %bitcast.101), channel_id=1, source_target_pairs={{8,0},{16,8},{24,16},{32,24},{40,32},{48,40},{56,48},{64,56},{72,6... | collective-permute-start | bytes 24584 | tf_op jit(solution)/shard_map/ppermute | solution.py:19
  10.4 7.8 %collective-permute-start = (f32[1,1,32,64]{3,2,1,0:T(8,128)S(1)}, f32[1,1,32,64]{3,2,1,0:T(8,128)S(1)}, u32[]{:S(2)}, u32[]{:S(2)}) collective-permute-start(f32[1,1,32,64]{3,2,1,0:T(8,128)S(1)} %bitcast.102), channel_id=1, source_target_pairs={{0,8},{8,16},{16,24},{24,32},{32,40},{40,48},{48,56},{56,64},{64,7... | collective-permute-start | bytes 24584 | tf_op jit(solution)/shard_map/ppermute | solution.py:17
  18.2 7.4 %collective-permute-start.3 = (f32[3,1,32,64]{3,2,1,0:T(8,128)S(1)}, f32[3,1,32,64]{3,2,1,0:T(8,128)S(1)}, u32[]{:S(2)}, u32[]{:S(2)}) collective-permute-start(f32[3,1,32,64]{3,2,1,0:T(8,128)S(1)} %pad_maximum_fusion.7), channel_id=1, source_target_pairs={{1,0},{2,1},{3,2},{4,3},{5,4},{6,5},{7,6},{9,8},{10,9},{11,10},{12... | collective-permute-start | bytes 73736 | tf_op jit(solution)/shard_map/ppermute | solution.py:19
  22.3 4.3 collective-permute-start.2
  26.8 5.3 collective-permute-start.5
  28.7 7.8 %collective-permute-start.4 = (f32[1,1,32,64]{3,2,1,0:T(8,128)S(1)}, f32[1,1,32,64]{3,2,1,0:T(8,128)S(1)}, u32[]{:S(2)}, u32[]{:S(2)}) collective-permute-start(f32[1,1,32,64]{3,2,1,0:T(8,128)S(1)} %convolution_bitcast_fusion.2), channel_id=1, source_target_pairs={{0,8},{8,16},{16,24},{24,32},{32,40},{40,48},{48,56},{56,64},{64,7... | collective-permute-start | bytes 24584 | tf_op jit(solution)/shard_map/ppermute | solution.py:17
  36.5 7.3 %collective-permute-start.7 = (f32[3,1,32,64]{3,2,1,0:T(8,128)S(1)}, f32[3,1,32,64]{3,2,1,0:T(8,128)S(1)}, u32[]{:S(2)}, u32[]{:S(2)}) collective-permute-start(f32[3,1,32,64]{3,2,1,0:T(8,128)S(1)} %pad_maximum_fusion.8), channel_id=1, source_target_pairs={{1,0},{2,1},{3,2},{4,3},{5,4},{6,5},{7,6},{9,8},{10,9},{11,10},{12... | collective-permute-start | bytes 73736 | tf_op jit(solution)/shard_map/ppermute | solution.py:19
  38.6 6.4 %collective-permute-start.6 = (f32[3,1,32,64]{3,2,1,0:T(8,128)S(1)}, f32[3,1,32,64]{3,2,1,0:T(8,128)S(1)}, u32[]{:S(2)}, u32[]{:S(2)}) collective-permute-start(f32[3,1,32,64]{3,2,1,0:T(8,128)S(1)} %pad_maximum_fusion.8), channel_id=1, source_target_pairs={{0,1},{1,2},{2,3},{3,4},{4,5},{5,6},{6,7},{8,9},{9,10},{10,11},{11... | collective-permute-start | bytes 73736 | tf_op jit(solution)/shard_map/ppermute | solution.py:17
  201.5 42.9 %copy-start = (f32[32,64,512]{2,1,0:T(8,128)S(1)}, f32[32,64,512]{2,1,0:T(8,128)}, u32[]{:S(2)}) copy-start(f32[32,64,512]{2,1,0:T(8,128)} %param.8) | copy-start | bytes 12582916
  206.9 5.8 %collective-permute-start.9 = (f32[1,1,32,64]{3,2,1,0:T(8,128)S(1)}, f32[1,1,32,64]{3,2,1,0:T(8,128)S(1)}, u32[]{:S(2)}, u32[]{:S(2)}) collective-permute-start(f32[1,1,32,64]{3,2,1,0:T(8,128)S(1)} %bitcast.113), channel_id=1, source_target_pairs={{8,0},{16,8},{24,16},{32,24},{40,32},{48,40},{56,48},{64,56},{72,6... | collective-permute-start | bytes 24584 | tf_op jit(solution)/shard_map/ppermute | solution.py:19
  210.8 7.8 %collective-permute-start.8 = (f32[1,1,32,64]{3,2,1,0:T(8,128)S(1)}, f32[1,1,32,64]{3,2,1,0:T(8,128)S(1)}, u32[]{:S(2)}, u32[]{:S(2)}) collective-permute-start(f32[1,1,32,64]{3,2,1,0:T(8,128)S(1)} %bitcast.114), channel_id=1, source_target_pairs={{0,8},{8,16},{16,24},{24,32},{32,40},{40,48},{48,56},{56,64},{64,7... | collective-permute-start | bytes 24584 | tf_op jit(solution)/shard_map/ppermute | solution.py:17
  218.6 5.9 %collective-permute-start.11 = (f32[3,1,32,64]{3,2,1,0:T(8,128)S(1)}, f32[3,1,32,64]{3,2,1,0:T(8,128)S(1)}, u32[]{:S(2)}, u32[]{:S(2)}) collective-permute-start(f32[3,1,32,64]{3,2,1,0:T(8,128)S(1)} %pad_maximum_fusion.9), channel_id=1, source_target_pairs={{1,0},{2,1},{3,2},{4,3},{5,4},{6,5},{7,6},{9,8},{10,9},{11,10},{12... | collective-permute-start | bytes 73736 | tf_op jit(solution)/shard_map/ppermute | solution.py:19
  222.6 3.1 collective-permute-start.10
  226.0 5.3 collective-permute-start.13
  227.9 7.8 %collective-permute-start.12 = (f32[1,1,32,64]{3,2,1,0:T(8,128)S(1)}, f32[1,1,32,64]{3,2,1,0:T(8,128)S(1)}, u32[]{:S(2)}, u32[]{:S(2)}) collective-permute-start(f32[1,1,32,64]{3,2,1,0:T(8,128)S(1)} %convolution_bitcast_fusion.1), channel_id=1, source_target_pairs={{0,8},{8,16},{16,24},{24,32},{32,40},{40,48},{48,56},{56,64},{64,7... | collective-permute-start | bytes 24584 | tf_op jit(solution)/shard_map/ppermute | solution.py:17
  235.7 7.5 %collective-permute-start.15 = (f32[3,1,32,64]{3,2,1,0:T(8,128)S(1)}, f32[3,1,32,64]{3,2,1,0:T(8,128)S(1)}, u32[]{:S(2)}, u32[]{:S(2)}) collective-permute-start(f32[3,1,32,64]{3,2,1,0:T(8,128)S(1)} %pad_maximum_fusion.10), channel_id=1, source_target_pairs={{1,0},{2,1},{3,2},{4,3},{5,4},{6,5},{7,6},{9,8},{10,9},{11,10},{12... | collective-permute-start | bytes 73736 | tf_op jit(solution)/shard_map/ppermute | solution.py:19
  238.9 5.2 collective-permute-start.14
  396.9 43.3 %copy-start.1 = (f32[32,64,512]{2,1,0:T(8,128)S(1)}, f32[32,64,512]{2,1,0:T(8,128)}, u32[]{:S(2)}) copy-start(f32[32,64,512]{2,1,0:T(8,128)} %param.8) | copy-start | bytes 12582916
  402.4 6.2 %collective-permute-start.17 = (f32[1,1,32,64]{3,2,1,0:T(8,128)S(1)}, f32[1,1,32,64]{3,2,1,0:T(8,128)S(1)}, u32[]{:S(2)}, u32[]{:S(2)}) collective-permute-start(f32[1,1,32,64]{3,2,1,0:T(8,128)S(1)} %bitcast.109), channel_id=1, source_target_pairs={{8,0},{16,8},{24,16},{32,24},{40,32},{48,40},{56,48},{64,56},{72,6... | collective-permute-start | bytes 24584 | tf_op jit(solution)/shard_map/ppermute | solution.py:19
  406.6 7.8 %collective-permute-start.16 = (f32[1,1,32,64]{3,2,1,0:T(8,128)S(1)}, f32[1,1,32,64]{3,2,1,0:T(8,128)S(1)}, u32[]{:S(2)}, u32[]{:S(2)}) collective-permute-start(f32[1,1,32,64]{3,2,1,0:T(8,128)S(1)} %bitcast.110), channel_id=1, source_target_pairs={{0,8},{8,16},{16,24},{24,32},{32,40},{40,48},{48,56},{56,64},{64,7... | collective-permute-start | bytes 24584 | tf_op jit(solution)/shard_map/ppermute | solution.py:17
  414.5 5.9 %collective-permute-start.19 = (f32[3,1,32,64]{3,2,1,0:T(8,128)S(1)}, f32[3,1,32,64]{3,2,1,0:T(8,128)S(1)}, u32[]{:S(2)}, u32[]{:S(2)}) collective-permute-start(f32[3,1,32,64]{3,2,1,0:T(8,128)S(1)} %pad_maximum_fusion.11), channel_id=1, source_target_pairs={{1,0},{2,1},{3,2},{4,3},{5,4},{6,5},{7,6},{9,8},{10,9},{11,10},{12... | collective-permute-start | bytes 73736 | tf_op jit(solution)/shard_map/ppermute | solution.py:19
  418.5 3.1 collective-permute-start.18
  421.8 5.3 collective-permute-start.21
  423.7 7.8 %collective-permute-start.20 = (f32[1,1,32,64]{3,2,1,0:T(8,128)S(1)}, f32[1,1,32,64]{3,2,1,0:T(8,128)S(1)}, u32[]{:S(2)}, u32[]{:S(2)}) collective-permute-start(f32[1,1,32,64]{3,2,1,0:T(8,128)S(1)} %convolution_bitcast_fusion), channel_id=1, source_target_pairs={{0,8},{8,16},{16,24},{24,32},{32,40},{40,48},{48,56},{56,64},{64,7... | collective-permute-start | bytes 24584 | tf_op jit(solution)/shard_map/ppermute | solution.py:17
  431.6 7.3 %collective-permute-start.23 = (f32[3,1,32,64]{3,2,1,0:T(8,128)S(1)}, f32[3,1,32,64]{3,2,1,0:T(8,128)S(1)}, u32[]{:S(2)}, u32[]{:S(2)}) collective-permute-start(f32[3,1,32,64]{3,2,1,0:T(8,128)S(1)} %pad_maximum_fusion.12), channel_id=1, source_target_pairs={{1,0},{2,1},{3,2},{4,3},{5,4},{6,5},{7,6},{9,8},{10,9},{11,10},{12... | collective-permute-start | bytes 73736 | tf_op jit(solution)/shard_map/ppermute | solution.py:19
  434.8 5.2 collective-permute-start.22
  440.2 88.9 %copy-start.7 = (s32[1024]{0:T(1024)S(1)}, s32[1024]{0:T(1024)}, u32[]{:S(2)}) copy-start(s32[1024]{0:T(1024)} %param.11) | copy-start | bytes 12292
  440.3 102.2 %copy-start.5 = (f32[64,1024]{1,0:T(8,128)S(1)}, f32[64,1024]{1,0:T(8,128)}, u32[]{:S(2)}) copy-start(f32[64,1024]{1,0:T(8,128)} %param.10) | copy-start | bytes 786436
  518.2 41.5 %copy-start.4 = (f32[32,512]{1,0:T(8,128)}, f32[32,512]{1,0:T(8,128)S(1)}, u32[]{:S(2)}) copy-start(f32[32,512]{1,0:T(8,128)S(1)} %get-tuple-element.12) | copy-start | bytes 196612
  523.5 5.6 %collective-permute-start.25 = (f32[1,1,32,64]{3,2,1,0:T(8,128)S(1)}, f32[1,1,32,64]{3,2,1,0:T(8,128)S(1)}, u32[]{:S(2)}, u32[]{:S(2)}) collective-permute-start(f32[1,1,32,64]{3,2,1,0:T(8,128)S(1)} %bitcast.105), channel_id=1, source_target_pairs={{8,0},{16,8},{24,16},{32,24},{40,32},{48,40},{56,48},{64,56},{72,6... | collective-permute-start | bytes 24584 | tf_op jit(solution)/shard_map/ppermute | solution.py:19
  527.2 7.8 %collective-permute-start.24 = (f32[1,1,32,64]{3,2,1,0:T(8,128)S(1)}, f32[1,1,32,64]{3,2,1,0:T(8,128)S(1)}, u32[]{:S(2)}, u32[]{:S(2)}) collective-permute-start(f32[1,1,32,64]{3,2,1,0:T(8,128)S(1)} %bitcast.106), channel_id=1, source_target_pairs={{0,8},{8,16},{16,24},{24,32},{32,40},{40,48},{48,56},{56,64},{64,7... | collective-permute-start | bytes 24584 | tf_op jit(solution)/shard_map/ppermute | solution.py:17
  535.0 7.7 %collective-permute-start.27 = (f32[3,1,32,64]{3,2,1,0:T(8,128)S(1)}, f32[3,1,32,64]{3,2,1,0:T(8,128)S(1)}, u32[]{:S(2)}, u32[]{:S(2)}) collective-permute-start(f32[3,1,32,64]{3,2,1,0:T(8,128)S(1)} %pad_maximum_fusion.13), channel_id=1, source_target_pairs={{1,0},{2,1},{3,2},{4,3},{5,4},{6,5},{7,6},{9,8},{10,9},{11,10},{12... | collective-permute-start | bytes 73736 | tf_op jit(solution)/shard_map/ppermute | solution.py:19
  539.0 4.6 collective-permute-start.26
where the time goes:
time: 563 us; the launch traced here: 561 us
  blocking collectives  381 us (68%)
  starting transfers between devices  87.6 us (16%)
  waiting for transfers between devices  43.8 us (8%)
  matrix products  32 us (6%)
  between operations  7.94 us (1%)
    psum x3, blocking collectives, squares(): return lax.psum(jnp.sum(values * values), ('gx', 'gy'))  221 us
    psum x2, blocking collectives, per_device(): alpha = norm_now / lax.psum(jnp.sum(direction * image), ('gx', 'gy'))  146 us
    ppermute x14, starting transfers between devices, with_halo(): lax.ppermute(head, axis, [((i + 1) % count, i) for i in range(ends)])  45.9 us
    ppermute x14, waiting for transfers between devices, with_halo(): lax.ppermute(tail, axis, [(i, (i + 1) % count) for i in range(ends)])  43.8 us
    ppermute x14, starting transfers between devices, with_halo(): lax.ppermute(tail, axis, [(i, (i + 1) % count) for i in range(ends)])  41.7 us
    dot_general x4, matrix products, coefficient(): jnp.einsum('bfv,bv->bf', features, field, precision=lax.Precision.HIGHEST)  22 us
    all_gather x1, blocking collectives, per_device(): slab_rows = lax.all_gather(surface, 'gy', axis=0, tiled=True)  13.1 us
  transfers between devices with their start and end apart: 28, of which 14 were waited for; matrix products, arithmetic and copies ran while one was open for 0% of the time, Pallas kernels for 0%

commit v1 on v0

--- a/solution.py
+++ b/solution.py
@@ -4,6 +4,11 @@
 from jax.sharding import PartitionSpec as P
 
 ITERS = 3
+
+
+def gather_by_exchange(value, axis, dim):
+    copies = jnp.concatenate([value] * lax.axis_size(axis), axis=dim)
+    return lax.all_to_all(copies, axis, dim, dim, tiled=True)
 
 
 def with_halo(cells, sides, width):
@@ -78,7 +83,7 @@
         direction = residual + norm_next / norm_now * direction
         norm_now = norm_next
     surface = first_sum(coefficient(features, solution_field))
-    slab_rows = lax.all_gather(surface, "gy", axis=0, tiled=True)
+    slab_rows = gather_by_exchange(surface, "gy", 0)
     local_ids = vertex_bricks - row_index * across * nrows
     picked = jnp.take(slab_rows, local_ids, axis=0)
     vertex_values = jnp.sum(vertex_features * picked.T, axis=0)

time: 563 us -> 562 us (level)
  blocking collectives: 381 us -> 368 us
    all_gather x1 -> x0, blocking collectives: 13.1 us -> none  [per_device(): slab_rows = lax.all_gather(surface, 'gy', axis=0, tiled=True)]
  transfers between devices with their start and end apart: 28 -> 29, of which waited for: 14 -> 15; matrix products, arithmetic and copies ran while one was open for 0% -> 0% of each run, Pallas kernels for 0% -> 0%
where the time goes in v1:
time: 562 us; the launch traced here: 559 us
  blocking collectives  368 us (65%)
  starting transfers between devices  92.1 us (16%)
  waiting for transfers between devices  48.7 us (9%)
  matrix products  32 us (6%)
  between operations  8 us (1%)
  other arithmetic  6.12 us (1%)
    psum x3, blocking collectives, squares(): return lax.psum(jnp.sum(values * values), ('gx', 'gy'))  221 us
    psum x2, blocking collectives, per_device(): alpha = norm_now / lax.psum(jnp.sum(direction * image), ('gx', 'gy'))  146 us
    ppermute x14, starting transfers between devices, with_halo(): lax.ppermute(head, axis, [((i + 1) % count, i) for i in range(ends)])  45.9 us
    ppermute x14, waiting for transfers between devices, with_halo(): lax.ppermute(tail, axis, [(i, (i + 1) % count) for i in range(ends)])  44 us
    ppermute x14, starting transfers between devices, with_halo(): lax.ppermute(tail, axis, [(i, (i + 1) % count) for i in range(ends)])  41.7 us
    dot_general x4, matrix products, coefficient(): jnp.einsum('bfv,bv->bf', features, field, precision=lax.Precision.HIGHEST)  22 us
  transfers between devices with their start and end apart: 29, of which 15 were waited for; matrix products, arithmetic and copies ran while one was open for 0% of the time, Pallas kernels for 0%

profile of v1, /device:TPU:129, one launch (start us, length us, event | category | flops | bytes accessed | tf_op | source)
XLA Modules:
  0.0 559.1 jit_solution(10469760436399397898)
XLA Ops:
  0.7 5.8 %fusion.8 = f32[32,1,64]{2,1,0:T(1,128)S(1)} fusion(f32[32,64,512]{2,1,0:T(8,128)} %param.8, f32[32,512,1]{1,0,2:T(8,128)} %bitcast.95), kind=kOutput, calls=%fused_computation.25 | convolution fusion | flops 12582912 | bytes 4268032 | tf_op jit(solution)/shard_map/bfv,bv->bf/dot_general | solution.py:32
  6.5 3.9 collective-permute-start.1
  10.4 1.9 collective-permute-start
  12.7 5.6 collective-permute-done
  18.2 4.0 collective-permute-start.3
  22.3 3.1 collective-permute-start.2
  25.7 0.8 collective-permute-done.2
  26.8 1.9 collective-permute-start.5
  28.7 3.4 collective-permute-start.4
  32.1 4.4 collective-permute-done.4
  36.5 2.1 collective-permute-start.7
  38.6 5.2 collective-permute-start.6
  43.8 1.1 collective-permute-done.6
  45.2 4.3 fusion.25
  49.5 0.6 multiply_reduce_fusion.4
  50.2 74.5 %all-reduce = (f32[]{:T(128)}, f32[]{:T(128)}) all-reduce(f32[]{:T(128)} %get-tuple-element.4, f32[]{:T(128)} %get-tuple-element.3), channel_id=1, replica_groups=mesh['gx'=32,'gy'=8] {'gx','gy'}, use_global_device_ids=true, to_apply=%region_1.2 | all-reduce | flops 2 | bytes 16 | tf_op jit(solution)/shard_map/psum | solution.py:36
  126.0 0.6 multiply_reduce_fusion.3
  126.7 73.5 %psum.44 = f32[]{:T(128)} all-reduce(f32[]{:T(128)} %get-tuple-element.9), channel_id=1, replica_groups=mesh['gx'=32,'gy'=8] {'gx','gy'}, use_global_device_ids=true, to_apply=%region_6.7 | all-reduce | flops 1 | bytes 8 | tf_op jit(solution)/shard_map/psum | solution.py:36
  201.5 5.4 fusion.6
  206.9 3.8 collective-permute-start.9
  210.8 1.9 collective-permute-start.8
  212.7 5.9 %collective-permute-done.8 = f32[1,1,32,64]{3,2,1,0:T(8,128)S(1)} collective-permute-done((f32[1,1,32,64]{3,2,1,0:T(8,128)S(1)}, f32[1,1,32,64]{3,2,1,0:T(8,128)S(1)}, u32[]{:S(2)}, u32[]{:S(2)}) %collective-permute-start.8) | collective-permute-done | bytes 8224 | tf_op jit(solution)/shard_map/ppermute | solution.py:22
  218.6 4.0 collective-permute-start.11
  222.6 1.9 collective-permute-start.10
  224.5 1.2 collective-permute-done.10
  226.0 1.9 collective-permute-start.13
  227.9 3.4 collective-permute-start.12
  231.3 4.4 collective-permute-done.12
  235.7 3.2 collective-permute-start.15
  238.9 4.3 collective-permute-start.14
  243.2 1.0 collective-permute-done.14
  244.4 2.1 fusion.27
  247.1 73.2 %psum.45 = f32[]{:T(128)} all-reduce(f32[]{:T(128)} %multiply_reduce_fusion.2), channel_id=1, replica_groups=mesh['gx'=32,'gy'=8] {'gx','gy'}, use_global_device_ids=true, to_apply=%region_8.9 | all-reduce | flops 1 | bytes 8 | tf_op jit(solution)/shard_map/psum | solution.py:79
  321.7 0.6 multiply_reduce_fusion.1
  322.3 73.3 %psum.46 = f32[]{:T(128)} all-reduce(f32[]{:T(128)} %get-tuple-element.7), channel_id=1, replica_groups=mesh['gx'=32,'gy'=8] {'gx','gy'}, use_global_device_ids=true, to_apply=%region_10.11 | all-reduce | flops 1 | bytes 8 | tf_op jit(solution)/shard_map/psum | solution.py:36
  397.0 5.4 fusion.4
  402.4 4.2 collective-permute-start.17
  406.6 1.9 collective-permute-start.16
  408.6 5.9 %collective-permute-done.16 = f32[1,1,32,64]{3,2,1,0:T(8,128)S(1)} collective-permute-done((f32[1,1,32,64]{3,2,1,0:T(8,128)S(1)}, f32[1,1,32,64]{3,2,1,0:T(8,128)S(1)}, u32[]{:S(2)}, u32[]{:S(2)}) %collective-permute-start.16) | collective-permute-done | bytes 8224 | tf_op jit(solution)/shard_map/ppermute | solution.py:22
  414.4 4.0 collective-permute-start.19
  418.4 1.9 collective-permute-start.18
  420.4 1.2 collective-permute-done.18
  421.8 1.9 collective-permute-start.21
  423.7 3.4 collective-permute-start.20
  427.1 4.4 collective-permute-done.20
  431.5 3.2 collective-permute-start.23
  434.8 4.1 collective-permute-start.22
  438.8 1.1 collective-permute-done.22
  440.3 2.1 fusion.29
  443.0 73.2 %psum.47 = f32[]{:T(128)} all-reduce(f32[]{:T(128)} %multiply_reduce_fusion), channel_id=1, replica_groups=mesh['gx'=32,'gy'=8] {'gx','gy'}, use_global_device_ids=true, to_apply=%region_12.13 | all-reduce | flops 1 | bytes 8 | tf_op jit(solution)/shard_map/psum | solution.py:79
  517.5 0.7 multiply_subtract_fusion
  518.2 5.3 fusion.2
  523.5 3.7 collective-permute-start.25
  527.2 1.9 collective-permute-start.24
  529.1 5.9 %collective-permute-done.24 = f32[1,1,32,64]{3,2,1,0:T(8,128)S(1)} collective-permute-done((f32[1,1,32,64]{3,2,1,0:T(8,128)S(1)}, f32[1,1,32,64]{3,2,1,0:T(8,128)S(1)}, u32[]{:S(2)}, u32[]{:S(2)}) %collective-permute-start.24) | collective-permute-done | bytes 8224 | tf_op jit(solution)/shard_map/ppermute | solution.py:22
  535.0 4.0 collective-permute-start.27
  539.0 3.4 collective-permute-start.26
  542.5 1.1 collective-permute-done.26
  543.9 0.7 reshape.94
  544.7 4.4 all-to-all-start
  549.3 4.6 all-to-all-done
  554.5 0.8 reduce
  555.3 2.8 gather_fusion
  558.2 1.0 fusion.1
  (72 shorter events, 4.4 us)
Async XLA Ops:
  0.6 11.7 %copy-start.6 = (s32[32,27]{1,0:T(8,128)S(1)}, s32[32,27]{1,0:T(8,128)}, u32[]{:S(2)}) copy-start(s32[32,27]{1,0:T(8,128)} %param.9) | copy-start | bytes 10372
  0.6 48.9 %copy-start.2 = (f32[32,512]{1,0:T(8,128)S(1)}, f32[32,512]{1,0:T(8,128)}, u32[]{:S(2)}) copy-start(f32[32,512]{1,0:T(8,128)} %param.7) | copy-start | bytes 196612
  0.7 48.9 %copy-start.3 = (f32[32,512]{1,0:T(8,128)S(1)}, f32[32,512]{1,0:T(8,128)}, u32[]{:S(2)}) copy-start(f32[32,512]{1,0:T(8,128)} %param.6) | copy-start | bytes 196612
  6.5 6.2 %collective-permute-start.1 = (f32[1,1,32,64]{3,2,1,0:T(8,128)S(1)}, f32[1,1,32,64]{3,2,1,0:T(8,128)S(1)}, u32[]{:S(2)}, u32[]{:S(2)}) collective-permute-start(f32[1,1,32,64]{3,2,1,0:T(8,128)S(1)} %bitcast.105), channel_id=1, source_target_pairs={{8,0},{16,8},{24,16},{32,24},{40,32},{48,40},{56,48},{64,56},{72,6... | collective-permute-start | bytes 24584 | tf_op jit(solution)/shard_map/ppermute | solution.py:24
  10.4 7.8 %collective-permute-start = (f32[1,1,32,64]{3,2,1,0:T(8,128)S(1)}, f32[1,1,32,64]{3,2,1,0:T(8,128)S(1)}, u32[]{:S(2)}, u32[]{:S(2)}) collective-permute-start(f32[1,1,32,64]{3,2,1,0:T(8,128)S(1)} %bitcast.106), channel_id=1, source_target_pairs={{0,8},{8,16},{16,24},{24,32},{32,40},{40,48},{48,56},{56,64},{64,7... | collective-permute-start | bytes 24584 | tf_op jit(solution)/shard_map/ppermute | solution.py:22
  18.2 7.4 %collective-permute-start.3 = (f32[3,1,32,64]{3,2,1,0:T(8,128)S(1)}, f32[3,1,32,64]{3,2,1,0:T(8,128)S(1)}, u32[]{:S(2)}, u32[]{:S(2)}) collective-permute-start(f32[3,1,32,64]{3,2,1,0:T(8,128)S(1)} %pad_maximum_fusion.7), channel_id=1, source_target_pairs={{1,0},{2,1},{3,2},{4,3},{5,4},{6,5},{7,6},{9,8},{10,9},{11,10},{12... | collective-permute-start | bytes 73736 | tf_op jit(solution)/shard_map/ppermute | solution.py:24
  22.3 4.3 collective-permute-start.2
  26.8 5.3 collective-permute-start.5
  28.7 7.8 %collective-permute-start.4 = (f32[1,1,32,64]{3,2,1,0:T(8,128)S(1)}, f32[1,1,32,64]{3,2,1,0:T(8,128)S(1)}, u32[]{:S(2)}, u32[]{:S(2)}) collective-permute-start(f32[1,1,32,64]{3,2,1,0:T(8,128)S(1)} %convolution_bitcast_fusion.2), channel_id=1, source_target_pairs={{0,8},{8,16},{16,24},{24,32},{32,40},{40,48},{48,56},{56,64},{64,7... | collective-permute-start | bytes 24584 | tf_op jit(solution)/shard_map/ppermute | solution.py:22
  36.5 7.3 %collective-permute-start.7 = (f32[3,1,32,64]{3,2,1,0:T(8,128)S(1)}, f32[3,1,32,64]{3,2,1,0:T(8,128)S(1)}, u32[]{:S(2)}, u32[]{:S(2)}) collective-permute-start(f32[3,1,32,64]{3,2,1,0:T(8,128)S(1)} %pad_maximum_fusion.8), channel_id=1, source_target_pairs={{1,0},{2,1},{3,2},{4,3},{5,4},{6,5},{7,6},{9,8},{10,9},{11,10},{12... | collective-permute-start | bytes 73736 | tf_op jit(solution)/shard_map/ppermute | solution.py:24
  38.6 6.4 %collective-permute-start.6 = (f32[3,1,32,64]{3,2,1,0:T(8,128)S(1)}, f32[3,1,32,64]{3,2,1,0:T(8,128)S(1)}, u32[]{:S(2)}, u32[]{:S(2)}) collective-permute-start(f32[3,1,32,64]{3,2,1,0:T(8,128)S(1)} %pad_maximum_fusion.8), channel_id=1, source_target_pairs={{0,1},{1,2},{2,3},{3,4},{4,5},{5,6},{6,7},{8,9},{9,10},{10,11},{11... | collective-permute-start | bytes 73736 | tf_op jit(solution)/shard_map/ppermute | solution.py:22
  201.5 42.9 %copy-start = (f32[32,64,512]{2,1,0:T(8,128)S(1)}, f32[32,64,512]{2,1,0:T(8,128)}, u32[]{:S(2)}) copy-start(f32[32,64,512]{2,1,0:T(8,128)} %param.8) | copy-start | bytes 12582916
  206.9 5.8 %collective-permute-start.9 = (f32[1,1,32,64]{3,2,1,0:T(8,128)S(1)}, f32[1,1,32,64]{3,2,1,0:T(8,128)S(1)}, u32[]{:S(2)}, u32[]{:S(2)}) collective-permute-start(f32[1,1,32,64]{3,2,1,0:T(8,128)S(1)} %bitcast.117), channel_id=1, source_target_pairs={{8,0},{16,8},{24,16},{32,24},{40,32},{48,40},{56,48},{64,56},{72,6... | collective-permute-start | bytes 24584 | tf_op jit(solution)/shard_map/ppermute | solution.py:24
  210.8 7.8 %collective-permute-start.8 = (f32[1,1,32,64]{3,2,1,0:T(8,128)S(1)}, f32[1,1,32,64]{3,2,1,0:T(8,128)S(1)}, u32[]{:S(2)}, u32[]{:S(2)}) collective-permute-start(f32[1,1,32,64]{3,2,1,0:T(8,128)S(1)} %bitcast.118), channel_id=1, source_target_pairs={{0,8},{8,16},{16,24},{24,32},{32,40},{40,48},{48,56},{56,64},{64,7... | collective-permute-start | bytes 24584 | tf_op jit(solution)/shard_map/ppermute | solution.py:22
  218.6 5.9 %collective-permute-start.11 = (f32[3,1,32,64]{3,2,1,0:T(8,128)S(1)}, f32[3,1,32,64]{3,2,1,0:T(8,128)S(1)}, u32[]{:S(2)}, u32[]{:S(2)}) collective-permute-start(f32[3,1,32,64]{3,2,1,0:T(8,128)S(1)} %pad_maximum_fusion.9), channel_id=1, source_target_pairs={{1,0},{2,1},{3,2},{4,3},{5,4},{6,5},{7,6},{9,8},{10,9},{11,10},{12... | collective-permute-start | bytes 73736 | tf_op jit(solution)/shard_map/ppermute | solution.py:24
  222.6 3.1 collective-permute-start.10
  226.0 5.3 collective-permute-start.13
  227.9 7.8 %collective-permute-start.12 = (f32[1,1,32,64]{3,2,1,0:T(8,128)S(1)}, f32[1,1,32,64]{3,2,1,0:T(8,128)S(1)}, u32[]{:S(2)}, u32[]{:S(2)}) collective-permute-start(f32[1,1,32,64]{3,2,1,0:T(8,128)S(1)} %convolution_bitcast_fusion.1), channel_id=1, source_target_pairs={{0,8},{8,16},{16,24},{24,32},{32,40},{40,48},{48,56},{56,64},{64,7... | collective-permute-start | bytes 24584 | tf_op jit(solution)/shard_map/ppermute | solution.py:22
  235.7 7.5 %collective-permute-start.15 = (f32[3,1,32,64]{3,2,1,0:T(8,128)S(1)}, f32[3,1,32,64]{3,2,1,0:T(8,128)S(1)}, u32[]{:S(2)}, u32[]{:S(2)}) collective-permute-start(f32[3,1,32,64]{3,2,1,0:T(8,128)S(1)} %pad_maximum_fusion.10), channel_id=1, source_target_pairs={{1,0},{2,1},{3,2},{4,3},{5,4},{6,5},{7,6},{9,8},{10,9},{11,10},{12... | collective-permute-start | bytes 73736 | tf_op jit(solution)/shard_map/ppermute | solution.py:24
  238.9 5.2 collective-permute-start.14
  396.9 43.3 %copy-start.1 = (f32[32,64,512]{2,1,0:T(8,128)S(1)}, f32[32,64,512]{2,1,0:T(8,128)}, u32[]{:S(2)}) copy-start(f32[32,64,512]{2,1,0:T(8,128)} %param.8) | copy-start | bytes 12582916
  402.4 6.2 %collective-permute-start.17 = (f32[1,1,32,64]{3,2,1,0:T(8,128)S(1)}, f32[1,1,32,64]{3,2,1,0:T(8,128)S(1)}, u32[]{:S(2)}, u32[]{:S(2)}) collective-permute-start(f32[1,1,32,64]{3,2,1,0:T(8,128)S(1)} %bitcast.113), channel_id=1, source_target_pairs={{8,0},{16,8},{24,16},{32,24},{40,32},{48,40},{56,48},{64,56},{72,6... | collective-permute-start | bytes 24584 | tf_op jit(solution)/shard_map/ppermute | solution.py:24
  406.6 7.8 %collective-permute-start.16 = (f32[1,1,32,64]{3,2,1,0:T(8,128)S(1)}, f32[1,1,32,64]{3,2,1,0:T(8,128)S(1)}, u32[]{:S(2)}, u32[]{:S(2)}) collective-permute-start(f32[1,1,32,64]{3,2,1,0:T(8,128)S(1)} %bitcast.114), channel_id=1, source_target_pairs={{0,8},{8,16},{16,24},{24,32},{32,40},{40,48},{48,56},{56,64},{64,7... | collective-permute-start | bytes 24584 | tf_op jit(solution)/shard_map/ppermute | solution.py:22
  414.4 5.9 %collective-permute-start.19 = (f32[3,1,32,64]{3,2,1,0:T(8,128)S(1)}, f32[3,1,32,64]{3,2,1,0:T(8,128)S(1)}, u32[]{:S(2)}, u32[]{:S(2)}) collective-permute-start(f32[3,1,32,64]{3,2,1,0:T(8,128)S(1)} %pad_maximum_fusion.11), channel_id=1, source_target_pairs={{1,0},{2,1},{3,2},{4,3},{5,4},{6,5},{7,6},{9,8},{10,9},{11,10},{12... | collective-permute-start | bytes 73736 | tf_op jit(solution)/shard_map/ppermute | solution.py:24
  418.4 3.1 collective-permute-start.18
  421.8 5.3 collective-permute-start.21
  423.7 7.8 %collective-permute-start.20 = (f32[1,1,32,64]{3,2,1,0:T(8,128)S(1)}, f32[1,1,32,64]{3,2,1,0:T(8,128)S(1)}, u32[]{:S(2)}, u32[]{:S(2)}) collective-permute-start(f32[1,1,32,64]{3,2,1,0:T(8,128)S(1)} %convolution_bitcast_fusion), channel_id=1, source_target_pairs={{0,8},{8,16},{16,24},{24,32},{32,40},{40,48},{48,56},{56,64},{64,7... | collective-permute-start | bytes 24584 | tf_op jit(solution)/shard_map/ppermute | solution.py:22
  431.5 7.3 %collective-permute-start.23 = (f32[3,1,32,64]{3,2,1,0:T(8,128)S(1)}, f32[3,1,32,64]{3,2,1,0:T(8,128)S(1)}, u32[]{:S(2)}, u32[]{:S(2)}) collective-permute-start(f32[3,1,32,64]{3,2,1,0:T(8,128)S(1)} %pad_maximum_fusion.12), channel_id=1, source_target_pairs={{1,0},{2,1},{3,2},{4,3},{5,4},{6,5},{7,6},{9,8},{10,9},{11,10},{12... | collective-permute-start | bytes 73736 | tf_op jit(solution)/shard_map/ppermute | solution.py:24
  434.8 5.2 collective-permute-start.22
  440.2 102.2 %copy-start.7 = (s32[1024]{0:T(1024)S(1)}, s32[1024]{0:T(1024)}, u32[]{:S(2)}) copy-start(s32[1024]{0:T(1024)} %param.11) | copy-start | bytes 12292
  440.2 108.9 %copy-start.5 = (f32[64,1024]{1,0:T(8,128)S(1)}, f32[64,1024]{1,0:T(8,128)}, u32[]{:S(2)}) copy-start(f32[64,1024]{1,0:T(8,128)} %param.10) | copy-start | bytes 786436
  518.2 40.0 %copy-start.4 = (f32[32,512]{1,0:T(8,128)}, f32[32,512]{1,0:T(8,128)S(1)}, u32[]{:S(2)}) copy-start(f32[32,512]{1,0:T(8,128)S(1)} %get-tuple-element.12) | copy-start | bytes 196612
  523.5 5.6 %collective-permute-start.25 = (f32[1,1,32,64]{3,2,1,0:T(8,128)S(1)}, f32[1,1,32,64]{3,2,1,0:T(8,128)S(1)}, u32[]{:S(2)}, u32[]{:S(2)}) collective-permute-start(f32[1,1,32,64]{3,2,1,0:T(8,128)S(1)} %bitcast.109), channel_id=1, source_target_pairs={{8,0},{16,8},{24,16},{32,24},{40,32},{48,40},{56,48},{64,56},{72,6... | collective-permute-start | bytes 24584 | tf_op jit(solution)/shard_map/ppermute | solution.py:24
  527.2 7.8 %collective-permute-start.24 = (f32[1,1,32,64]{3,2,1,0:T(8,128)S(1)}, f32[1,1,32,64]{3,2,1,0:T(8,128)S(1)}, u32[]{:S(2)}, u32[]{:S(2)}) collective-permute-start(f32[1,1,32,64]{3,2,1,0:T(8,128)S(1)} %bitcast.110), channel_id=1, source_target_pairs={{0,8},{8,16},{16,24},{24,32},{32,40},{40,48},{48,56},{56,64},{64,7... | collective-permute-start | bytes 24584 | tf_op jit(solution)/shard_map/ppermute | solution.py:22
  535.0 7.5 %collective-permute-start.27 = (f32[3,1,32,64]{3,2,1,0:T(8,128)S(1)}, f32[3,1,32,64]{3,2,1,0:T(8,128)S(1)}, u32[]{:S(2)}, u32[]{:S(2)}) collective-permute-start(f32[3,1,32,64]{3,2,1,0:T(8,128)S(1)} %pad_maximum_fusion.13), channel_id=1, source_target_pairs={{1,0},{2,1},{3,2},{4,3},{5,4},{6,5},{7,6},{9,8},{10,9},{11,10},{12... | collective-permute-start | bytes 73736 | tf_op jit(solution)/shard_map/ppermute | solution.py:24
  539.0 4.6 collective-permute-start.26
  544.7 9.3 %all-to-all-start = ((f32[8,1,2048]{2,1,0:T(1,128)}), f32[8,1,2048]{2,1,0:T(1,128)S(1)}, u32[]{:S(2)}, u32[]{:S(2)}) async-start(f32[8,1,2048]{2,1,0:T(1,128)} %reshape.94), calls=%async_computation | async-start | bytes 131072 | tf_op jit(solution)/shard_map/all_to_all | solution.py:11
